TPU v7x, 32 devices: a whole 2x2x4 slice. The times are simulated.
32 devices in a mesh: section: 8 (over y, x, core), fsdp: 4 (over z).
Axes of the slice: x: 2, y: 2, z: 4, core: 2. Of those that a mesh axis runs over, the one named last changes fastest.
Arguments:
- layer_input: bfloat16 [8, 512, 4096], P('section', 'fsdp'), may hold values from -6 to 6
- next_cot: bfloat16 [8, 512, 512], P('section', 'fsdp'), may hold values from -6 to 6
- w_value: bfloat16 [8, 4096, 512], P('section', 'fsdp'), may hold values from -0.25 to 0.25
- micro_ids: int32 [8, 4], P('section', 'fsdp'), may hold values from 0 to 1
Outputs:
- grad_input: bfloat16 [8, 512, 4096], P('section', 'fsdp')
- grad_sum: float32 [8, 4096, 512], P('section', 'fsdp')
- grad_square: float32 [8, 4096, 512], P('section', 'fsdp')
All inputs are finite; a program needn't handle non-finite values.
Results may differ from a plain program's by a relative error of at most 0.0037.
Values may be sent and summed in bfloat16 or wider, within the bound.
A program may use at most 64 MiB of HBM per device.

v0:
```python
import jax
import jax.numpy as jnp
from jax import lax
from jax.sharding import PartitionSpec as P

MICRO = 2


def from_behind(value, axis, steps):
    count = lax.axis_size(axis)
    pairs = [(source, (source + steps) % count) for source in range(count)]
    return lax.ppermute(value, axis, pairs)


def body(layer_input, next_cot, w_value, micro_ids):
    inputs_local = layer_input[0]
    incoming = from_behind(next_cot, "section", -1)[0]
    weight_local = w_value[0]
    fsdp_count = lax.axis_size("fsdp")
    token_count = inputs_local.shape[0]
    row_share = weight_local.shape[0]
    columns = weight_local.shape[1]
    inverse = 1.0 / token_count
    owned = lax.all_to_all(inputs_local, "fsdp", split_axis=1, concat_axis=0, tiled=True)
    cot_all, micro_all = (
        lax.all_gather(incoming, "fsdp", axis=0, tiled=True),
        lax.all_gather(micro_ids, "fsdp", axis=1, tiled=True),
    )
    owner_cols = lax.dot_general(
        cot_all, weight_local, (((1,), (1,)), ((), ())), preferred_element_type=jnp.float32
    ).astype(jnp.bfloat16)
    grad_input = lax.all_to_all(owner_cols, "fsdp", split_axis=0, concat_axis=1, tiled=True)
    owned = owned.reshape(fsdp_count, token_count, row_share)
    cot_blocks = cot_all.reshape(fsdp_count, token_count, columns)
    partial_value = (
        jnp.einsum("ftd,ftc->fdc", owned, cot_blocks, preferred_element_type=jnp.float32) * inverse
    )
    partial_value = lax.optimization_barrier(partial_value.astype(jnp.bfloat16)).astype(jnp.float32)
    onehot = (micro_all[0][:, None] == jnp.arange(MICRO, dtype=jnp.int32)[None, :]).astype(
        jnp.float32
    )
    stacked = jnp.einsum("fm,fdc->mdc", onehot, partial_value)
    grad_sum = jnp.sum(stacked, axis=0)
    grad_square = jnp.sum(stacked * stacked, axis=0)
    return (grad_input[None], grad_sum[None], grad_square[None])


def solution(mesh):
    return jax.shard_map(
        body,
        mesh=mesh,
        in_specs=(
            P("section", "fsdp", None),
            P("section", "fsdp", None),
            P("section", "fsdp", None),
            P("section", "fsdp"),
        ),
        out_specs=(
            P("section", "fsdp", None),
            P("section", "fsdp", None),
            P("section", "fsdp", None),
        ),
        check_vma=False,
    )
```

profile of v0, /device:TPU:0, one launch (start us, length us, event | category | flops | bytes accessed | tf_op | source)
XLA Modules:
  0.0 94.9 jit_solution(13938566455108437013)
XLA Ops:
  0.6 0.0 copy-start
  0.6 0.0 copy-start.2
  0.7 1.7 %copy.10 = bf16[1,128,4096]{1,2,0:T(8,128)(2,1)S(1)} copy(bf16[1,128,4096]{2,1,0:T(8,128)(2,1)} %param.4) | data formatting | bytes 2097152 | tf_op args[0]
  2.4 1.3 %copy.11 = bf16[128,4,1024]{2,0,1:T(8,128)(2,1)} copy(bf16[128,4,1024]{0,2,1:T(8,128)(2,1)S(1)} %bitcast.25) | data formatting | bytes 2097152 | tf_op jit(solution)/shard_map/all_to_all | solution.py:24
  3.7 6.5 %all-to-all-start.1 = ((bf16[128,4,1024]{2,0,1:T(8,128)(2,1)}), bf16[128,4,1024]{2,0,1:T(8,128)(2,1)S(1)}, u32[]{:S(2)}, u32[]{:S(2)}) async-start(bf16[128,4,1024]{2,0,1:T(8,128)(2,1)} %copy.11), calls=%async_computation.1 | async-start | bytes 2097152 | tf_op jit(solution)/shard_map/all_to_all | solution.py:24
  10.2 0.0 copy-done.2
  10.2 1.6 %collective-permute-start = (bf16[1,128,512]{2,1,0:T(8,128)(2,1)S(1)}, bf16[1,128,512]{2,1,0:T(8,128)(2,1)S(1)}, u32[]{:S(2)}, u32[]{:S(2)}) collective-permute-start(bf16[1,128,512]{2,1,0:T(8,128)(2,1)S(1)} %copy-done.2), channel_id=1, source_target_pairs={{0,28},{4,0},{8,4},{12,8},{16,12},{20,16},{24,20},{28,24},{1,29},{... | collective-permute-start | bytes 393224 | tf_op jit(solution)/shard_map/ppermute | solution.py:12
  11.8 2.5 %collective-permute-done = bf16[1,128,512]{2,1,0:T(8,128)(2,1)S(1)} collective-permute-done((bf16[1,128,512]{2,1,0:T(8,128)(2,1)S(1)}, bf16[1,128,512]{2,1,0:T(8,128)(2,1)S(1)}, u32[]{:S(2)}, u32[]{:S(2)}) %collective-permute-start) | collective-permute-done | bytes 131104 | tf_op jit(solution)/shard_map/ppermute | solution.py:12
  14.3 32.0 %all-gather = bf16[1,512,512]{2,1,0:T(8,128)(2,1)S(1)} all-gather(bf16[1,128,512]{2,1,0:T(8,128)(2,1)S(1)} %collective-permute-done), channel_id=2, replica_groups=mesh['section'=8,'fsdp'=4] {'fsdp'}, dimensions={1}, use_global_device_ids=true | all-gather | bytes 655360 | tf_op jit(solution)/shard_map/all_gather | solution.py:26
  46.3 0.8 copy-done.1
  47.1 0.0 copy-done
  47.1 1.7 %convolution_convert_fusion = bf16[512,1024]{1,0:T(8,128)(2,1)} fusion(bf16[1,1024,512]{2,1,0:T(8,128)(2,1)S(1)} %copy-done, bf16[1,512,512]{2,1,0:T(8,128)(2,1)S(1)} %all-gather), kind=kOutput, calls=%fused_computation.4 | convolution fusion | flops 537395200 | bytes 2621440 | tf_op jit(solution)/shard_map/dot_general | solution.py:29
  48.8 0.0 all-to-all-done.1
  48.8 4.6 %all-to-all-start = ((bf16[4,128,1024]{2,1,0:T(8,128)(2,1)}), bf16[4,128,1024]{2,1,0:T(8,128)(2,1)S(1)}, u32[]{:S(2)}, u32[]{:S(2)}) async-start(bf16[4,128,1024]{2,1,0:T(8,128)(2,1)} %bitcast.27), calls=%async_computation | async-start | bytes 2097152 | tf_op jit(solution)/shard_map/all_to_all | solution.py:32
  54.1 0.0 copy-done.3
  54.1 0.6 dynamic-slice
  54.7 0.7 bitcast_dynamic-update-slice_fusion
  55.3 20.2 %all-reduce = s32[4]{0:T(128)S(1)} all-reduce(s32[4]{0:T(128)S(1)} %bitcast_dynamic-update-slice_fusion), channel_id=1, replica_groups=mesh['section'=8,'fsdp'=4] {'fsdp'}, use_global_device_ids=true, to_apply=%add | all-reduce | flops 4 | bytes 32
  75.6 1.3 %copy.12 = bf16[128,4,1024]{0,2,1:T(8,128)(2,1)} copy(bf16[128,4,1024]{2,0,1:T(8,128)(2,1)S(1)} %all-to-all-done.1) | data formatting | bytes 2097152 | tf_op jit(solution)/shard_map/all_to_all | solution.py:24
  76.9 2.6 %multiply_convert_fusion = bf16[4,1024,512]{2,1,0:T(8,128)(2,1)S(1)} fusion(bf16[4,128,512]{2,1,0:T(8,128)(2,1)} %bitcast.26, bf16[128,4,1024]{0,2,1:T(8,128)(2,1)} %copy.12), kind=kOutput, calls=%fused_computation | convolution fusion | flops 541065216 | bytes 5767168 | tf_op jit(solution)/shard_map/ftd,ftc->fdc/dot_general | solution.py:36
  79.4 13.0 %multiply_reduce_fusion = (f32[1024,512]{1,0:T(8,128)}, f32[1024,512]{1,0:T(8,128)}) fusion(bf16[4,1024,512]{2,1,0:T(8,128)(2,1)S(1)} %multiply_convert_fusion, s32[4]{0:T(128)S(1)} %all-reduce), kind=kOutput, calls=%fused_computation.1 | convolution fusion | flops 10485768 | bytes 8388624 | tf_op jit(solution)/shard_map/fm,fdc->mdc/dot_general | solution.py:42
  92.5 0.0 all-to-all-done
  92.5 0.8 copy.9
  93.3 1.6 %broadcast_in_dim.10 = bf16[1,128,4096]{2,1,0:T(8,128)(2,1)} reshape(bf16[128,4,1024]{2,1,0:T(4,128)(2,1)S(1)} %copy.9) | data formatting | bytes 2097152 | tf_op jit(solution)/shard_map/broadcast_in_dim | solution.py:45
  (3 shorter events, 0.0 us)
Async XLA Ops:
  0.6 46.5 %copy-start = (bf16[1,1024,512]{2,1,0:T(8,128)(2,1)S(1)}, bf16[1,1024,512]{2,1,0:T(8,128)(2,1)}, u32[]{:S(2)}) copy-start(bf16[1,1024,512]{2,1,0:T(8,128)(2,1)} %param.6) | copy-start | bytes 3145732
  0.6 9.5 %copy-start.2 = (bf16[1,128,512]{2,1,0:T(8,128)(2,1)S(1)}, bf16[1,128,512]{2,1,0:T(8,128)(2,1)}, u32[]{:S(2)}) copy-start(bf16[1,128,512]{2,1,0:T(8,128)(2,1)} %param.5) | copy-start | bytes 393220
  3.7 50.4 %copy-start.3 = (u32[32]{0:T(128)S(1)}, u32[32]{0:T(128)}, u32[]{:S(2)}) copy-start(u32[32]{0:T(128)} %constant.10) | copy-start | bytes 388
  3.7 45.1 %all-to-all-start.1 = ((bf16[128,4,1024]{2,0,1:T(8,128)(2,1)}), bf16[128,4,1024]{2,0,1:T(8,128)(2,1)S(1)}, u32[]{:S(2)}, u32[]{:S(2)}) async-start(bf16[128,4,1024]{2,0,1:T(8,128)(2,1)} %copy.11), calls=%async_computation.1 | async-start | bytes 2097152 | tf_op jit(solution)/shard_map/all_to_all | solution.py:24
  10.2 4.1 %collective-permute-start = (bf16[1,128,512]{2,1,0:T(8,128)(2,1)S(1)}, bf16[1,128,512]{2,1,0:T(8,128)(2,1)S(1)}, u32[]{:S(2)}, u32[]{:S(2)}) collective-permute-start(bf16[1,128,512]{2,1,0:T(8,128)(2,1)S(1)} %copy-done.2), channel_id=1, source_target_pairs={{0,28},{4,0},{8,4},{12,8},{16,12},{20,16},{24,20},{28,24},{1,29},{... | collective-permute-start | bytes 393224 | tf_op jit(solution)/shard_map/ppermute | solution.py:12
  46.3 0.8 copy-start.1
  48.8 43.7 %all-to-all-start = ((bf16[4,128,1024]{2,1,0:T(8,128)(2,1)}), bf16[4,128,1024]{2,1,0:T(8,128)(2,1)S(1)}, u32[]{:S(2)}, u32[]{:S(2)}) async-start(bf16[4,128,1024]{2,1,0:T(8,128)(2,1)} %bitcast.27), calls=%async_computation | async-start | bytes 2097152 | tf_op jit(solution)/shard_map/all_to_all | solution.py:32
where the time goes:
time: 95.2 us; the launch traced here: 94.9 us
  blocking collectives  52.2 us (55%)
  matrix products  17.4 us (18%)
  starting transfers between devices  12.7 us (13%)
  local copies, waits for them, and re-layouts  8.82 us (9%)
  waiting for transfers between devices  2.53 us (3%)
  between operations  1.34 us (1%)
    all_gather x1, blocking collectives, body(): lax.all_gather(incoming, 'fsdp', axis=0, tiled=True)  32 us
    unnamed x1, blocking collectives  20.2 us
    dot_general x1, matrix products, body(): stacked = jnp.einsum('fm,fdc->mdc', onehot, partial_value)  13 us
    all_to_all x1, starting transfers between devices, body(): lax.all_to_all(inputs_local, 'fsdp', split_axis=1, concat_axis=0, tiled=T...  6.48 us
    all_to_all x1, starting transfers between devices, body(): lax.all_to_all(owner_cols, 'fsdp', split_axis=0, concat_axis=1, tiled=True)  4.58 us
    unnamed x12, local copies, waits for them, and re-layouts  3.8 us
    all_to_all x2, local copies, waits for them, and re-layouts, body(): lax.all_to_all(inputs_local, 'fsdp', split_axis=1, concat_axis=0, tiled=T...  2.61 us
    dot_general x1, matrix products, body(): jnp.einsum('ftd,ftc->fdc', owned, cot_blocks, preferred_element_type=jnp....  2.59 us
  transfers between devices with their start and end apart: 3, of which 1 were waited for; matrix products, arithmetic and copies ran while one was open for 21% of the time, Pallas kernels for 0%

commit v1 on v0

--- a/solution.py
+++ b/solution.py
@@ -1,9 +1,21 @@
+import functools
 import jax
 import jax.numpy as jnp
 from jax import lax
 from jax.sharding import PartitionSpec as P
 
 MICRO = 2
+
+
+def _follow_sums_all(mine, join_dim, at_axis):
+    low = lax.axis_size("fsdp")
+    block_out = jnp.split(mine, low, join_dim)
+    w1 = jnp.stack(block_out, 0)
+    mixed_arr = lax.all_to_all(w1, "fsdp", 0, 0)
+    return jnp.concatenate(mixed_arr, at_axis)
+
+
+shape_the_limits = functools.partial(_follow_sums_all, join_dim=1, at_axis=0)
 
 
 def from_behind(value, axis, steps):
@@ -21,7 +33,7 @@
     row_share = weight_local.shape[0]
     columns = weight_local.shape[1]
     inverse = 1.0 / token_count
-    owned = lax.all_to_all(inputs_local, "fsdp", split_axis=1, concat_axis=0, tiled=True)
+    owned = shape_the_limits(inputs_local)
     cot_all, micro_all = (
         lax.all_gather(incoming, "fsdp", axis=0, tiled=True),
         lax.all_gather(micro_ids, "fsdp", axis=1, tiled=True),

time: 95.2 us -> 83.5 us (0.88)
  blocking collectives: 52.2 us -> 38.3 us
  other arithmetic: 0 us -> 7.04 us
  local copies, waits for them, and re-layouts: 8.82 us -> 6.28 us
  matrix products: 17.4 us -> 15.5 us
    all_gather x1, blocking collectives: 32 us -> 15.9 us  [body(): lax.all_gather(incoming, 'fsdp', axis=0, tiled=True)]
    convert_element_type x0 -> x1, other arithmetic: none -> 5.93 us  [body(): partial_value.astype(jnp.bfloat16)]
    all_to_all x2 -> x0, local copies, waits for them, and re-layouts: 2.61 us -> none  [body(): lax.all_to_all(inputs_local, 'fsdp', split_axis=1, concat_axis=0, tiled=T...]
    unnamed x12 -> x9, local copies, waits for them, and re-layouts: 3.8 us -> 1.28 us
    ppermute x1, waiting for transfers between devices: 2.52 us -> 0.01 us  [from_behind(): return lax.ppermute(value, axis, pairs)]
    all_to_all x1, waiting for transfers between devices: 0.01 us -> 2.48 us  [body(): lax.all_to_all(owner_cols, 'fsdp', split_axis=0, concat_axis=1, tiled=True)]
    unnamed x1, blocking collectives: 20.2 us -> 22.4 us
    another operation x0 -> x1, local copies, waits for them, and re-layouts: none -> 1.38 us  [_follow_sums_all(): w1 = jnp.stack(block_out, 0)]
  transfers between devices with their start and end apart: 3 -> 3, of which waited for: 1 -> 1; matrix products, arithmetic and copies ran while one was open for 21% -> 27% of each run, Pallas kernels for 0% -> 0%
where the time goes in v1:
time: 83.5 us; the launch traced here: 83.1 us
  blocking collectives  38.3 us (46%)
  matrix products  15.5 us (19%)
  starting transfers between devices  12.2 us (15%)
  other arithmetic  7.04 us (8%)
  local copies, waits for them, and re-layouts  6.28 us (8%)
  waiting for transfers between devices  2.49 us (3%)
  between operations  1.36 us (2%)
    unnamed x1, blocking collectives  22.4 us
    all_gather x1, blocking collectives, body(): lax.all_gather(incoming, 'fsdp', axis=0, tiled=True)  15.9 us
    dot_general x1, matrix products, body(): stacked = jnp.einsum('fm,fdc->mdc', onehot, partial_value)  12.5 us
    all_to_all x1, starting transfers between devices, _follow_sums_all(): mixed_arr = lax.all_to_all(w1, 'fsdp', 0, 0)  6.35 us
    convert_element_type x1, other arithmetic, body(): partial_value.astype(jnp.bfloat16)  5.93 us
    all_to_all x1, starting transfers between devices, body(): lax.all_to_all(owner_cols, 'fsdp', split_axis=0, concat_axis=1, tiled=True)  4.23 us
    all_to_all x1, waiting for transfers between devices, body(): lax.all_to_all(owner_cols, 'fsdp', split_axis=0, concat_axis=1, tiled=True)  2.48 us
    all_to_all x1, local copies, waits for them, and re-layouts, body(): lax.all_to_all(owner_cols, 'fsdp', split_axis=0, concat_axis=1, tiled=True)  2.04 us
  transfers between devices with their start and end apart: 3, of which 1 were waited for; matrix products, arithmetic and copies ran while one was open for 27% of the time, Pallas kernels for 0%

profile of v1, /device:TPU:0, one launch (start us, length us, event | category | flops | bytes accessed | tf_op | source)
XLA Modules:
  0.0 83.1 jit_solution(13408158782730606754)
XLA Ops:
  0.6 0.0 copy-start
  0.6 0.0 copy-start.2
  0.7 0.0 copy-start.1
  0.7 1.4 %slice_bitcast_fusion.3 = (bf16[1,128,1024]{2,1,0:T(8,128)(2,1)S(1)}, bf16[1,128,1024]{2,1,0:T(8,128)(2,1)S(1)}, bf16[1,128,1024]{2,1,0:T(8,128)(2,1)S(1)}, bf16[1,128,1024]{2,1,0:T(8,128)(2,1)S(1)}) fusion(bf16[128,4096]{1,0:T(8,128)(2,1)} %bitcast.32), kind=kLoop, calls=%fused_computation.10 | loop fusion | bytes 2097152 | tf_op jit(solution)/shard_map/stack | solution.py:13
  2.0 1.1 %pad_maximum_fusion = bf16[4,128,1024]{2,1,0:T(8,128)(2,1)} fusion(bf16[1,128,1024]{2,1,0:T(8,128)(2,1)S(1)} %get-tuple-element.6, bf16[1,128,1024]{2,1,0:T(8,128)(2,1)S(1)} %get-tuple-element.7, bf16[1,128,1024]{2,1,0:T(8,128)(2,1)S(1)} %get-tuple-element.8, bf16[1,128,1024]{2,1,0:T(8,128)(2,1)S(1)} %get-tuple-element.5), kind=kLoop, calls=%fused_computation.4 | loop fusion | flops 1572864 | bytes 2097152 | tf_op jit(solution)/shard_map/stack | solution.py:13
  3.2 6.3 %all-to-all-start.1 = ((bf16[4,128,1024]{2,1,0:T(8,128)(2,1)}), bf16[4,128,1024]{2,1,0:T(8,128)(2,1)S(1)}, u32[]{:S(2)}, u32[]{:S(2)}) async-start(bf16[4,128,1024]{2,1,0:T(8,128)(2,1)} %pad_maximum_fusion), calls=%async_computation.1 | async-start | bytes 2097152 | tf_op jit(solution)/shard_map/all_to_all | solution.py:14
  9.5 0.0 copy-done.1
  9.5 1.6 %collective-permute-start = (bf16[1,128,512]{2,1,0:T(8,128)(2,1)S(1)}, bf16[1,128,512]{2,1,0:T(8,128)(2,1)S(1)}, u32[]{:S(2)}, u32[]{:S(2)}) collective-permute-start(bf16[1,128,512]{2,1,0:T(8,128)(2,1)S(1)} %copy-done.1), channel_id=1, source_target_pairs={{0,28},{4,0},{8,4},{12,8},{16,12},{20,16},{24,20},{28,24},{1,29},{... | collective-permute-start | bytes 393224 | tf_op jit(solution)/shard_map/ppermute | solution.py:24
  11.8 0.0 copy-done.2
  11.8 0.6 dynamic-slice
  12.4 0.7 bitcast_dynamic-update-slice_fusion
  13.0 22.4 %all-reduce = s32[4]{0:T(128)S(1)} all-reduce(s32[4]{0:T(128)S(1)} %bitcast_dynamic-update-slice_fusion), channel_id=1, replica_groups=mesh['section'=8,'fsdp'=4] {'fsdp'}, use_global_device_ids=true, to_apply=%add | all-reduce | flops 4 | bytes 32
  35.4 0.0 collective-permute-done
  35.4 15.9 %all-gather = bf16[1,512,512]{2,1,0:T(8,128)(2,1)S(1)} all-gather(bf16[1,128,512]{2,1,0:T(8,128)(2,1)S(1)} %collective-permute-done), channel_id=2, replica_groups=mesh['section'=8,'fsdp'=4] {'fsdp'}, dimensions={1}, use_global_device_ids=true | all-gather | bytes 655360 | tf_op jit(solution)/shard_map/all_gather | solution.py:38
  51.3 0.0 copy-done
  51.3 1.7 %convolution_convert_fusion = bf16[512,1024]{1,0:T(8,128)(2,1)} fusion(bf16[1,1024,512]{2,1,0:T(8,128)(2,1)S(1)} %copy-done, bf16[1,512,512]{2,1,0:T(8,128)(2,1)S(1)} %all-gather), kind=kOutput, calls=%fused_computation.3 | convolution fusion | flops 537395200 | bytes 2621440 | tf_op jit(solution)/shard_map/dot_general | solution.py:41
  53.0 0.0 all-to-all-done.1
  53.0 4.2 %all-to-all-start = ((bf16[4,128,1024]{2,1,0:T(8,128)(2,1)}), bf16[4,128,1024]{2,1,0:T(8,128)(2,1)}, u32[]{:S(2)}, u32[]{:S(2)}) async-start(bf16[4,128,1024]{2,1,0:T(8,128)(2,1)} %bitcast.33), calls=%async_computation | async-start | bytes 2097152 | tf_op jit(solution)/shard_map/all_to_all | solution.py:44
  57.3 1.3 %fusion.8 = f32[4,1024,512]{2,1,0:T(8,128)S(1)} fusion(bf16[4,128,1024]{2,1,0:T(8,128)(2,1)S(1)} %all-to-all-done.1, bf16[4,128,512]{2,1,0:T(8,128)(2,1)S(1)} %bitcast.31), kind=kOutput, calls=%fused_computation.17 | convolution fusion | flops 536870912 | bytes 9961472 | tf_op jit(solution)/shard_map/ftd,ftc->fdc/dot_general | solution.py:48
  58.6 5.9 %fusion = bf16[4,1024,512]{2,0,1:T(4,128)(2,1)S(1)} fusion(f32[4,1024,512]{2,1,0:T(8,128)S(1)} %fusion.8), kind=kLoop, calls=%fused_computation.1 | loop fusion | flops 4194304 | bytes 12582912 | tf_op jit(solution)/shard_map/convert_element_type | solution.py:50
  64.5 12.5 %multiply_reduce_fusion = (f32[1024,512]{1,0:T(8,128)}, f32[1024,512]{1,0:T(8,128)}) fusion(bf16[4,1024,512]{2,0,1:T(4,128)(2,1)S(1)} %fusion, s32[4]{0:T(128)S(1)} %all-reduce), kind=kOutput, calls=%fused_computation.2 | convolution fusion | flops 10485768 | bytes 8388624 | tf_op jit(solution)/shard_map/fm,fdc->mdc/dot_general | solution.py:54
  77.0 2.5 %all-to-all-done = bf16[4,128,1024]{2,1,0:T(8,128)(2,1)} async-done(((bf16[4,128,1024]{2,1,0:T(8,128)(2,1)}), bf16[4,128,1024]{2,1,0:T(8,128)(2,1)}, u32[]{:S(2)}, u32[]{:S(2)}) %all-to-all-start) | async-done | bytes 1048608 | tf_op jit(solution)/shard_map/all_to_all | solution.py:44
  79.5 2.0 %copy.7 = bf16[128,4,1024]{2,1,0:T(4,128)(2,1)S(1)} copy(bf16[128,4,1024]{2,0,1:T(8,128)(2,1)} %bitcast.3) | data formatting | bytes 2097152 | tf_op jit(solution)/shard_map/all_to_all | solution.py:44
  81.5 1.6 %broadcast_in_dim.10 = bf16[1,128,4096]{2,1,0:T(8,128)(2,1)} reshape(bf16[128,4,1024]{2,1,0:T(4,128)(2,1)S(1)} %copy.7) | data formatting | bytes 2097152 | tf_op jit(solution)/shard_map/broadcast_in_dim | solution.py:57
  (1 shorter events, 0.0 us)
Async XLA Ops:
  0.6 50.7 %copy-start = (bf16[1,1024,512]{2,1,0:T(8,128)(2,1)S(1)}, bf16[1,1024,512]{2,1,0:T(8,128)(2,1)}, u32[]{:S(2)}) copy-start(bf16[1,1024,512]{2,1,0:T(8,128)(2,1)} %param.6) | copy-start | bytes 3145732
  0.6 11.1 %copy-start.2 = (u32[32]{0:T(128)S(1)}, u32[32]{0:T(128)}, u32[]{:S(2)}) copy-start(u32[32]{0:T(128)} %constant.10) | copy-start | bytes 388
  0.7 8.8 %copy-start.1 = (bf16[1,128,512]{2,1,0:T(8,128)(2,1)S(1)}, bf16[1,128,512]{2,1,0:T(8,128)(2,1)}, u32[]{:S(2)}) copy-start(bf16[1,128,512]{2,1,0:T(8,128)(2,1)} %param.5) | copy-start | bytes 393220
  3.2 49.9 %all-to-all-start.1 = ((bf16[4,128,1024]{2,1,0:T(8,128)(2,1)}), bf16[4,128,1024]{2,1,0:T(8,128)(2,1)S(1)}, u32[]{:S(2)}, u32[]{:S(2)}) async-start(bf16[4,128,1024]{2,1,0:T(8,128)(2,1)} %pad_maximum_fusion), calls=%async_computation.1 | async-start | bytes 2097152 | tf_op jit(solution)/shard_map/all_to_all | solution.py:14
  9.5 25.9 %collective-permute-start = (bf16[1,128,512]{2,1,0:T(8,128)(2,1)S(1)}, bf16[1,128,512]{2,1,0:T(8,128)(2,1)S(1)}, u32[]{:S(2)}, u32[]{:S(2)}) collective-permute-start(bf16[1,128,512]{2,1,0:T(8,128)(2,1)S(1)} %copy-done.1), channel_id=1, source_target_pairs={{0,28},{4,0},{8,4},{12,8},{16,12},{20,16},{24,20},{28,24},{1,29},{... | collective-permute-start | bytes 393224 | tf_op jit(solution)/shard_map/ppermute | solution.py:24
  53.0 26.5 %all-to-all-start = ((bf16[4,128,1024]{2,1,0:T(8,128)(2,1)}), bf16[4,128,1024]{2,1,0:T(8,128)(2,1)}, u32[]{:S(2)}, u32[]{:S(2)}) async-start(bf16[4,128,1024]{2,1,0:T(8,128)(2,1)} %bitcast.33), calls=%async_computation | async-start | bytes 2097152 | tf_op jit(solution)/shard_map/all_to_all | solution.py:44
